TPU v7x, 32 devices: a whole 2x2x4 slice. The times are simulated.
32 devices in a mesh: rows: 8 (over y, x, core), cols: 4 (over z).
Axes of the slice: x: 2, y: 2, z: 4, core: 2. Of those that a mesh axis runs over, the one named last changes fastest.
Arguments:
- grads: bfloat16 [9216, 8192], P(('rows', 'cols')), may hold values from -6 to 6
- tests: float32 [64, 8192], P(None, 'cols'), may hold values from -6 to 6
Outputs:
- solution: float32 [64, 8192], P(None, 'cols')
- scores: float32 [64, 9216], P(None, ('rows', 'cols'))
All inputs are finite; a program needn't handle non-finite values.
Results may differ from a plain program's by a relative error of at most 0.0041.
Values may be sent and summed in bfloat16 or wider, within the bound.
A program may use at most 64 MiB of HBM per device.

v0:
```python
import jax
import jax.numpy as jnp
from jax import lax
from jax.sharding import PartitionSpec as P

ITERS = 2


damping = 0.5


def per_device(grads, tests):
    n_rows = lax.axis_size("rows")
    n_cols = lax.axis_size("cols")
    n_total = grads.shape[0] * n_rows * n_cols
    width = grads.shape[1]
    solution = jnp.zeros(tests.shape, jnp.float32)
    residual = tests
    direction = tests
    norm_now = lax.psum(jnp.sum(residual * residual, axis=1), "cols")
    for step in range(ITERS):
        proj = lax.dot_general(
            grads,
            lax.all_gather(direction.astype(jnp.bfloat16), "cols", axis=1, tiled=True),
            (((1,), (1,)), ((), ())),
            preferred_element_type=jnp.float32,
        ).astype(jnp.bfloat16)
        partial_value = lax.dot_general(
            proj, grads, (((0,), (0,)), ((), ())), preferred_element_type=jnp.float32
        )
        owned = lax.psum_scatter(partial_value, "cols", scatter_dimension=1, tiled=True)
        owned = lax.psum(owned, "rows")
        image = owned / n_total + damping * direction
        curv, cross, image_sq = lax.psum(
            (
                jnp.sum(direction * image, axis=1),
                jnp.sum(residual * image, axis=1),
                jnp.sum(image * image, axis=1),
            ),
            "cols",
        )
        alpha = norm_now / curv
        norm_next = norm_now - 2.0 * alpha * cross + alpha * alpha * image_sq
        solution = solution + alpha[:, None] * direction
        residual = residual - alpha[:, None] * image
        if step + 1 < ITERS:
            direction = residual + (norm_next / norm_now)[:, None] * direction
            norm_now = norm_next
    scores = lax.dot_general(
        lax.all_gather(solution.astype(jnp.bfloat16), "cols", axis=1, tiled=True),
        grads,
        (((1,), (1,)), ((), ())),
        preferred_element_type=jnp.float32,
    )
    return (solution, scores * width ** (-0.5))


def solution(mesh):
    placed = (P(("rows", "cols"), None), P(None, "cols"))
    return jax.shard_map(
        per_device,
        mesh=mesh,
        in_specs=placed,
        out_specs=(P(None, "cols"), P(None, ("rows", "cols"))),
        check_vma=False,
    )
```

profile of v0, /device:TPU:0, one launch (start us, length us, event | category | flops | bytes accessed | tf_op | source)
XLA Modules:
  0.0 350.8 jit_solution(4595125535650454993)
XLA Ops:
  7.2 0.0 all-gather.4.cloned.1.call-start
  7.2 1.8 convert_element_type.16
  9.0 0.0 all-gather.4.cloned.1.call-update
  9.0 0.0 copy-start
  9.0 0.0 reduce-scatter.3.cloned.1.call-start
  9.1 31.8 %all-gather.4.cloned.1.call-done = bf16[64,8192]{1,0:T(8,128)(2,1)} async-done(((bf16[64,2048]{1,0:T(8,128)(2,1)}), bf16[64,8192]{1,0:T(8,128)(2,1)}) %all-gather.4.cloned.1.call-update) | async-done | bytes 1048592 | tf_op jit(solution)/shard_map/all_gather | solution.py:24
  40.9 9.4 %fusion = f32[64,8192]{1,0:T(8,128)} fusion(bf16[288,8192]{1,0:T(8,128)(2,1)} %param.2, bf16[64,8192]{1,0:T(8,128)(2,1)} %all-gather.4.cloned.1.call-done), kind=kOutput, calls=%fused_computation.2 | convolution fusion | flops 603998208 | bytes 7864320 | tf_op jit(solution)/shard_map/dot_general | solution.py:28
  50.3 0.0 reduce-scatter.3.cloned.1.call-update
  50.3 0.0 all-reduce.4.cloned.1.call-start
  50.4 43.1 %reduce-scatter.3.cloned.1.call-done = f32[64,2048]{1,0:T(8,128)} async-done(((f32[64,8192]{1,0:T(8,128)}), f32[64,2048]{1,0:T(8,128)}) %reduce-scatter.3.cloned.1.call-update) | async-done | bytes 524304 | tf_op jit(solution)/shard_map/reduce_scatter | solution.py:31
  93.5 0.0 all-reduce.4.cloned.1.call-update
  93.5 0.0 all-gather.6.cloned.1.call-start
  93.5 57.1 %all-reduce.4.cloned.1.call-done = f32[64,2048]{1,0:T(8,128)} async-done(((f32[64,2048]{1,0:T(8,128)}), f32[64,2048]{1,0:T(8,128)}) %all-reduce.4.cloned.1.call-update) | async-done | bytes 524304 | tf_op jit(solution)/shard_map/psum | solution.py:32
  150.6 0.0 copy-done
  150.6 1.3 multiply_reduce_fusion.2
  151.9 11.6 %all-reduce = (f32[64]{0:T(128)S(1)}, f32[64]{0:T(128)S(1)}, f32[64]{0:T(128)S(1)}) all-reduce(f32[64]{0:T(128)S(1)} %get-tuple-element.3, f32[64]{0:T(128)S(1)} %get-tuple-element.4, f32[64]{0:T(128)S(1)} %get-tuple-element.2), channel_id=1, replica_groups=mesh['rows'=8,'cols'=4] {'cols'}, use_global_device_ids=true, to_apply=%region_7.0 | all-reduce | flops 192 | bytes 1536 | tf_op jit(solution)/shard_map/psum | solution.py:34
  163.6 1.9 fusion.2
  165.5 0.0 all-gather.6.cloned.1.call-update
  165.5 0.0 copy-start.1
  165.5 0.0 reduce-scatter.5.cloned.1.call-start
  165.6 24.7 %all-gather.6.cloned.1.call-done = bf16[64,8192]{1,0:T(8,128)(2,1)} async-done(((bf16[64,2048]{1,0:T(8,128)(2,1)}), bf16[64,8192]{1,0:T(8,128)(2,1)}) %all-gather.6.cloned.1.call-update) | async-done | bytes 1048592 | tf_op jit(solution)/shard_map/all_gather | solution.py:24
  190.3 9.6 %fusion.1 = f32[64,8192]{1,0:T(8,128)} fusion(bf16[288,8192]{1,0:T(8,128)(2,1)} %param.2, bf16[64,8192]{1,0:T(8,128)(2,1)} %all-gather.6.cloned.1.call-done), kind=kOutput, calls=%fused_computation.4 | convolution fusion | flops 603998208 | bytes 7864320 | tf_op jit(solution)/shard_map/dot_general | solution.py:28
  199.9 0.0 reduce-scatter.5.cloned.1.call-update
  199.9 0.0 all-reduce.6.cloned.1.call-start
  199.9 43.1 %reduce-scatter.5.cloned.1.call-done = f32[64,2048]{1,0:T(8,128)} async-done(((f32[64,8192]{1,0:T(8,128)}), f32[64,2048]{1,0:T(8,128)}) %reduce-scatter.5.cloned.1.call-update) | async-done | bytes 524304 | tf_op jit(solution)/shard_map/reduce_scatter | solution.py:31
  243.1 0.0 all-reduce.6.cloned.1.call-update
  243.1 0.0 all-gather.8.cloned.1.call-start
  243.1 56.9 %all-reduce.6.cloned.1.call-done = f32[64,2048]{1,0:T(8,128)} async-done(((f32[64,2048]{1,0:T(8,128)}), f32[64,2048]{1,0:T(8,128)}) %all-reduce.6.cloned.1.call-update) | async-done | bytes 524304 | tf_op jit(solution)/shard_map/psum | solution.py:32
  300.0 0.0 copy-done.1
  300.1 1.4 multiply_reduce_fusion
  301.5 11.6 %psum.50 = f32[64]{0:T(128)S(1)} all-reduce(f32[64]{0:T(128)S(1)} %multiply_reduce_fusion), channel_id=1, replica_groups=mesh['rows'=8,'cols'=4] {'cols'}, use_global_device_ids=true, to_apply=%region_11.0 | all-reduce | flops 64 | bytes 512 | tf_op jit(solution)/shard_map/psum | solution.py:34
  313.1 1.1 fusion.3
  314.2 0.0 all-gather.8.cloned.1.call-update
  314.3 24.8 %all-gather.8.cloned.1.call-done = bf16[64,8192]{1,0:T(8,128)(2,1)} async-done(((bf16[64,2048]{1,0:T(8,128)(2,1)}), bf16[64,8192]{1,0:T(8,128)(2,1)}) %all-gather.8.cloned.1.call-update) | async-done | bytes 1048592 | tf_op jit(solution)/shard_map/all_gather | solution.py:50
  339.0 5.0 %convolution_multiply_fusion = f32[64,288]{1,0:T(8,128)} fusion(bf16[64,8192]{1,0:T(8,128)(2,1)} %all-gather.8.cloned.1.call-done, bf16[288,8192]{1,0:T(8,128)(2,1)} %param.2), kind=kOutput, calls=%fused_computation.1 | convolution fusion | flops 302008320 | bytes 5840896 | tf_op jit(solution)/shard_map/dot_general | solution.py:49
  (2 shorter events, 0.0 us)
Async XLA Ops:
  7.2 33.7 %all-gather.4.cloned.1.call-start = ((), (), s32[]{:S(2)}) async-start(), calls=%async_computation.2 | async-start | bytes 1310720 | tf_op jit(solution)/shard_map/all_gather | solution.py:24
  9.0 141.6 %copy-start = (f32[64,2048]{1,0:T(8,128)S(1)}, f32[64,2048]{1,0:T(8,128)}, u32[]{:S(2)}) copy-start(f32[64,2048]{1,0:T(8,128)} %param.3) | copy-start | bytes 1572868
  9.0 84.5 %reduce-scatter.3.cloned.1.call-start = ((), (), s32[]{:S(2)}) async-start(), calls=%async_computation.3 | async-start | bytes 2621440 | tf_op jit(solution)/shard_map/reduce_scatter | solution.py:31
  50.3 100.3 %all-reduce.4.cloned.1.call-start = ((), (), s32[]{:S(2)}) async-start(), calls=%async_computation.4 | async-start | bytes 1048576 | tf_op jit(solution)/shard_map/psum | solution.py:32
  93.5 96.8 %all-gather.6.cloned.1.call-start = ((), (), s32[]{:S(2)}) async-start(), calls=%async_computation.5 | async-start | bytes 1310720 | tf_op jit(solution)/shard_map/all_gather | solution.py:24
  165.5 134.5 %copy-start.1 = (f32[64,2048]{1,0:T(8,128)S(1)}, f32[64,2048]{1,0:T(8,128)}, u32[]{:S(2)}) copy-start(f32[64,2048]{1,0:T(8,128)} %all-reduce.4.cloned.1.call-done) | copy-start | bytes 1572868
  165.5 77.5 %reduce-scatter.5.cloned.1.call-start = ((), (), s32[]{:S(2)}) async-start(), calls=%async_computation.6 | async-start | bytes 2621440 | tf_op jit(solution)/shard_map/reduce_scatter | solution.py:31
  199.9 100.2 %all-reduce.6.cloned.1.call-start = ((), (), s32[]{:S(2)}) async-start(), calls=%async_computation.7 | async-start | bytes 1048576 | tf_op jit(solution)/shard_map/psum | solution.py:32
  243.1 95.9 %all-gather.8.cloned.1.call-start = ((), (), s32[]{:S(2)}) async-start(), calls=%async_computation.8 | async-start | bytes 1310720 | tf_op jit(solution)/shard_map/all_gather | solution.py:50
Sparse Core Ops, SparseCore 0:
  10.1 30.6 all-gather.3
  50.4 43.0 reduce-scatter.2
  96.6 53.9 all-reduce.3
  165.6 24.5 all-gather.5
  200.0 43.0 reduce-scatter.4
  246.0 53.9 all-reduce.5
  314.4 24.5 all-gather.7
where the time goes:
time: 351 us
  waiting for transfers between devices  282 us (80%)
  matrix products  24 us (7%)
  blocking collectives  23.2 us (7%)
  between operations  14.1 us (4%)
  other arithmetic  7.59 us (2%)
    psum x2, waiting for transfers between devices, per_device(): owned = lax.psum(owned, 'rows')  114 us
    reduce_scatter x2, waiting for transfers between devices, per_device(): lax.psum_scatter(partial_value, 'cols', scatter_dimension=1, tiled=True)  86.2 us
    all_gather x2, waiting for transfers between devices, per_device(): lax.all_gather(direction.astype(jnp.bfloat16), 'cols', axis=1, tiled=True)  56.5 us
    all_gather x1, waiting for transfers between devices, per_device(): lax.all_gather(solution.astype(jnp.bfloat16), 'cols', axis=1, tiled=True)  24.8 us
    psum x2, blocking collectives, per_device(): lax.psum((jnp.sum(direction * image, axis=1), jnp.sum(residual * image, a...  23.2 us
    dot_general x2, matrix products, per_device(): lax.dot_general(proj, grads, (((0,), (0,)), ((), ())), preferred_element_...  19 us
  transfers between devices with their start and end apart: 7, of which 7 were waited for; matrix products, arithmetic and copies ran while one was open for 0% of the time, Pallas kernels for 0%

commit v1 on v0

v1 whole, which is shorter than its diff:
```python
import jax
import jax.numpy as jnp
from jax import lax
from jax.sharding import PartitionSpec as P

damping = 0.5


def per_device(grads, tests):
    n_total = grads.shape[0] * lax.axis_size("rows") * lax.axis_size("cols")
    width = grads.shape[1]
    own = tests.shape[1]
    direction = lax.all_gather(tests, "cols", axis=1, tiled=True)
    norm_now = jnp.sum(direction * direction, axis=1)

    def project(d):
        return lax.dot_general(
            grads, d.astype(jnp.bfloat16), (((1,), (1,)), ((), ())), preferred_element_type=jnp.float32
        )

    partial_value = lax.dot_general(
        project(direction).astype(jnp.bfloat16), grads, (((0,), (0,)), ((), ())), preferred_element_type=jnp.float32
    )
    image = lax.psum(partial_value, ("rows", "cols")) / n_total + damping * direction
    alpha = norm_now / jnp.sum(direction * image, axis=1)
    solution = alpha[:, None] * direction
    residual = direction - alpha[:, None] * image
    norm_next = jnp.sum(residual * residual, axis=1)
    direction = residual + (norm_next / norm_now)[:, None] * direction
    proj = project(direction)
    curv = lax.psum(jnp.sum(proj * proj.astype(jnp.bfloat16).astype(jnp.float32), axis=0), ("rows", "cols"))
    curv = curv / n_total + damping * jnp.sum(direction * direction, axis=1)
    solution = solution + (norm_next / curv)[:, None] * direction
    scores = lax.dot_general(
        solution.astype(jnp.bfloat16), grads, (((1,), (1,)), ((), ())), preferred_element_type=jnp.float32
    )
    mine = lax.dynamic_slice_in_dim(solution, lax.axis_index("cols") * own, own, axis=1)
    return (mine, scores * width ** (-0.5))


def solution(mesh):
    placed = (P(("rows", "cols"), None), P(None, "cols"))
    return jax.shard_map(
        per_device,
        mesh=mesh,
        in_specs=placed,
        out_specs=(P(None, "cols"), P(None, ("rows", "cols"))),
        check_vma=False,
    )
```

time: 351 us -> 262 us (0.75)
  waiting for transfers between devices: 282 us -> 184 us
  blocking collectives: 23.2 us -> 38.9 us
  matrix products: 24 us -> 13.8 us
    reduce_scatter x2 -> x0, waiting for transfers between devices: 86.2 us -> none  [per_device(): lax.psum_scatter(partial_value, 'cols', scatter_dimension=1, tiled=True)]
    all_gather x3 -> x1, waiting for transfers between devices: 81.2 us -> 50 us  [per_device(): direction = lax.all_gather(tests, 'cols', axis=1, tiled=True)]
    psum x2 -> x1, waiting for transfers between devices: 114 us -> 134 us  [per_device(): lax.psum(partial_value, ('rows', 'cols')) / n_total + damping * direction]
    psum x2 -> x1, blocking collectives: 23.2 us -> 38.9 us  [per_device(): lax.psum(jnp.sum(proj * proj.astype(jnp.bfloat16).astype(jnp.float32), ax...]
    dot_general x3, matrix products: 24 us -> 13.8 us  [the longest x1 9.67 us: per_device(): lax.dot_general(project(direction).astype(jnp.bfloat16), grads, (((0,), (...]
    convert_element_type x3 -> x0, other arithmetic: 4.84 us -> none  [the longest x2 3.69 us: per_device(): direction.astype(jnp.bfloat16)]
    reduce_sum x2 -> x3, other arithmetic: 2.74 us -> 7.13 us  [the longest x1 2.49 us: per_device(): curv = curv / n_total + damping * jnp.sum(direction * direction, axis=1)]
  transfers between devices with their start and end apart: 7 -> 2, of which waited for: 7 -> 2; matrix products, arithmetic and copies ran while one was open for 0% -> 0% of each run, Pallas kernels for 0% -> 0%
where the time goes in v1:
time: 262 us
  waiting for transfers between devices  184 us (70%)
  blocking collectives  38.9 us (15%)
  between operations  14.1 us (5%)
  matrix products  13.8 us (5%)
  other arithmetic  9.47 us (4%)
    psum x1, waiting for transfers between devices, per_device(): lax.psum(partial_value, ('rows', 'cols')) / n_total + damping * direction  134 us
    all_gather x1, waiting for transfers between devices, per_device(): direction = lax.all_gather(tests, 'cols', axis=1, tiled=True)  50 us
    psum x1, blocking collectives, per_device(): lax.psum(jnp.sum(proj * proj.astype(jnp.bfloat16).astype(jnp.float32), ax...  38.9 us
    dot_general x1, matrix products, per_device(): lax.dot_general(project(direction).astype(jnp.bfloat16), grads, (((0,), (...  9.67 us
  transfers between devices with their start and end apart: 2, of which 2 were waited for; matrix products, arithmetic and copies ran while one was open for 0% of the time, Pallas kernels for 0%

profile of v1, /device:TPU:0, one launch (start us, length us, event | category | flops | bytes accessed | tf_op | source)
XLA Modules:
  0.0 261.7 jit_solution(16199284651384448593)
XLA Ops:
  7.2 0.0 all-gather.2.cloned.1.call-start
  7.2 0.7 all-gather.2.cloned.1.call-update
  7.9 0.0 all-reduce.2.cloned.1.call-start
  7.9 50.0 %all-gather.2.cloned.1.call-done = f32[64,8192]{1,0:T(8,128)} async-done(((f32[64,2048]{1,0:T(8,128)}), f32[64,8192]{1,0:T(8,128)}) %all-gather.2.cloned.1.call-update) | async-done | bytes 2097168 | tf_op jit(solution)/shard_map/all_gather | solution.py:13
  58.0 9.7 %fusion = f32[64,8192]{1,0:T(8,128)} fusion(bf16[288,8192]{1,0:T(8,128)(2,1)} %param.2, f32[64,8192]{1,0:T(8,128)} %all-gather.2.cloned.1.call-done), kind=kOutput, calls=%fused_computation.11 | convolution fusion | flops 604522496 | bytes 8912896 | tf_op jit(solution)/shard_map/dot_general | solution.py:21
  67.6 0.0 copy-start
  67.6 0.0 all-reduce.2.cloned.1.call-update
  67.7 133.7 %all-reduce.2.cloned.1.call-done = f32[64,8192]{1,0:T(8,128)} async-done(((f32[64,8192]{1,0:T(8,128)}), f32[64,8192]{1,0:T(8,128)}) %all-reduce.2.cloned.1.call-update) | async-done | bytes 2097168 | tf_op jit(solution)/shard_map/psum | solution.py:24
  201.4 0.0 copy-done
  201.4 0.0 copy-start.1
  201.4 2.3 multiply_reduce_fusion.2
  203.7 0.0 copy-start.2
  203.7 2.3 multiply_reduce_fusion.1
  206.1 0.0 copy-done.1
  206.1 0.0 copy-done.2
  206.1 0.0 slice-start
  206.1 1.8 multiply_reduce_fusion.4
  207.9 38.9 %psum.15 = f32[64]{0:T(128)S(1)} all-reduce(f32[64]{0:T(128)S(1)} %multiply_reduce_fusion.4), channel_id=1, replica_groups=mesh['rows'=8,'cols'=4] {'rows','cols'}, use_global_device_ids=true, to_apply=%region_5.0 | all-reduce | flops 64 | bytes 512 | tf_op jit(solution)/shard_map/psum | solution.py:31
  246.9 0.0 slice-start.1
  246.9 2.5 multiply_reduce_fusion
  249.4 2.3 multiply_add_fusion
  251.7 0.0 slice-done
  251.7 0.0 slice-done.1
  251.7 2.3 convolution_multiply_fusion
  254.0 0.8 constant_dynamic-slice_fusion
  (4 shorter events, 0.0 us)
Async XLA Ops:
  7.2 50.8 %all-gather.2.cloned.1.call-start = ((), (), s32[]{:S(2)}) async-start(), calls=%async_computation | async-start | bytes 2621440 | tf_op jit(solution)/shard_map/all_gather | solution.py:13
  7.9 193.5 %all-reduce.2.cloned.1.call-start = ((), (), s32[]{:S(2)}) async-start(), calls=%async_computation.1 | async-start | bytes 4194304 | tf_op jit(solution)/shard_map/psum | solution.py:24
  67.6 133.7 %copy-start = (f32[64,8192]{1,0:T(8,128)S(1)}, f32[64,8192]{1,0:T(8,128)}, u32[]{:S(2)}) copy-start(f32[64,8192]{1,0:T(8,128)} %all-gather.2.cloned.1.call-done) | copy-start | bytes 6291460
  201.4 4.7 %copy-start.1 = (bf16[288,8192]{1,0:T(8,128)(2,1)S(1)}, bf16[288,8192]{1,0:T(8,128)(2,1)}, u32[]{:S(2)}) copy-start(bf16[288,8192]{1,0:T(8,128)(2,1)} %param.2) | copy-start | bytes 14155780
  203.7 2.4 copy-start.2
  206.1 45.6 %slice-start = ((s8[4718592]{0:T(1024)(128)(4,1)}), s8[524288]{0:T(1024)(128)(4,1)S(1)}, s32[]{:S(2)}) async-start(s8[4718592]{0:T(1024)(128)(4,1)} %bitcast.8), calls=%async_computation.2 | async-start | bytes 1048576
  246.9 4.8 %slice-start.1 = ((s8[4718592]{0:T(1024)(128)(4,1)}), s8[4194304]{0:T(1024)(128)(4,1)S(1)}, s32[]{:S(2)}) async-start(s8[4718592]{0:T(1024)(128)(4,1)} %bitcast.8), calls=%async_computation.3 | async-start | bytes 8388608
Sparse Core Ops, SparseCore 0:
  9.5 48.3 all-gather.1
  67.8 133.5 all-reduce.1

commit v2 on v1

--- a/solution.py
+++ b/solution.py
@@ -1,12 +1,20 @@
+import functools
+
 import jax
 import jax.numpy as jnp
 from jax import lax
+from jax.experimental import pallas as pl
+from jax.experimental.pallas import tpu as pltpu
 from jax.sharding import PartitionSpec as P
 
+MESH = pl.DeviceIdType.MESH
+LANES = 2
+BLOCK = 1024
+
 damping = 0.5
 
 
-def per_device(grads, tests):
+def plain(grads, tests):
     n_total = grads.shape[0] * lax.axis_size("rows") * lax.axis_size("cols")
     width = grads.shape[1]
     own = tests.shape[1]
@@ -38,10 +46,267 @@
     return (mine, scores * width ** (-0.5))
 
 
+def bits_of(count):
+    return count.bit_length() - 1
+
+
+def reverse_bits(value, count):
+    out = 0
+    for _ in range(count):
+        out, value = out * 2 + value % 2, value // 2
+    return out
+
+
+def kernel(nr, nc, grads, tests, out, scores, g, t, acc, img, box, mail, load_sem, own_sem, send_sem, recv_sem, csend, crecv):
+    me = {"rows": lax.axis_index("rows"), "cols": lax.axis_index("cols")}
+    n = nr * nc
+    count, own = tests.shape
+    width = grads.shape[1]
+    chunk = width // n
+    n_total = grads.shape[0] * n
+    span = count // LANES
+    rest = list(range(1, bits_of(nr)))
+    low = [("cols", b) for b in range(bits_of(nc))]
+    orders = [[("rows", b) for b in [0] + r] + low for r in (rest, rest[::-1])]
+    stages = len(orders[0])
+
+    def bit(stage):
+        axis, b = stage
+        return lax.rem(lax.div(me[axis], 2**b), 2)
+
+    def partner(stage):
+        axis, b = stage
+        return {axis: me[axis] + (1 - 2 * bit(stage)) * 2**b}
+
+    loads = []
+    for v in range(n):
+        at = reverse_bits(v % nc, bits_of(nc)) * nr + v // nc
+        loads.append(
+            pltpu.make_async_copy(
+                grads.at[:, pl.ds(at * chunk, chunk)], g.at[:, pl.ds(v * chunk, chunk)], load_sem.at[v]
+            )
+        )
+        loads[-1].start()
+
+    rows = [pl.ds(lane * span, span) for lane in range(LANES)]
+    place = []
+    firsts = []
+    for lane, order in enumerate(orders):
+        v = 0
+        for stage in order:
+            v = v * 2 + bit(stage)
+        place.append(v)
+        copy = pltpu.make_async_copy(
+            tests.at[rows[lane], pl.ds(pl.multiple_of(lax.div(v, nc) * chunk, chunk), chunk)],
+            t.at[rows[lane], pl.ds(pl.multiple_of(v * chunk, chunk), chunk)],
+            own_sem.at[lane],
+        )
+        copy.start()
+        firsts.append(copy)
+
+    barrier = pltpu.get_barrier_semaphore()
+    for stage in orders[0]:
+        pl.semaphore_signal(barrier, inc=1, device_id=partner(stage), device_id_type=MESH)
+    pl.semaphore_wait(barrier, stages)
+
+    def gather(buf, phase, ready):
+        sent = []
+        start = list(place)
+        flying = [None] * LANES
+        for k in range(stages):
+            size = chunk * 2**k
+            for lane in range(LANES):
+                stage = orders[lane][stages - 1 - k]
+                if k == 0:
+                    ready(lane)
+                else:
+                    flying[lane].wait_recv()
+                part = buf.at[rows[lane], pl.ds(pl.multiple_of(start[lane] * chunk, size), size)]
+                flying[lane] = pltpu.make_async_remote_copy(
+                    src_ref=part,
+                    dst_ref=part,
+                    send_sem=send_sem.at[phase, lane, k],
+                    recv_sem=recv_sem.at[phase, lane, k],
+                    device_id=partner(stage),
+                    device_id_type=MESH,
+                )
+                flying[lane].start()
+                sent.append(flying[lane])
+                start[lane] = start[lane] - bit(stage) * 2**k
+        for copy in flying:
+            copy.wait_recv()
+        return sent
+
+    def scatter(phase):
+        sent = []
+        start = [0] * LANES
+        flying = [None] * LANES
+        offset = 0
+        for k in range(stages + 1):
+            half = width // 2 ** (k + 1)
+            for lane in range(LANES):
+                if k:
+                    flying[lane].wait_recv()
+                    at = pl.ds(pl.multiple_of(start[lane], 2 * half), 2 * half)
+                    acc[rows[lane], at] = acc[rows[lane], at] + box[rows[lane], pl.ds(offset - 2 * half, 2 * half)]
+                if k < stages:
+                    stage = orders[lane][k]
+                    give = start[lane] + (1 - bit(stage)) * half
+                    start[lane] = start[lane] + bit(stage) * half
+                    flying[lane] = pltpu.make_async_remote_copy(
+                        src_ref=acc.at[rows[lane], pl.ds(pl.multiple_of(give, half), half)],
+                        dst_ref=box.at[rows[lane], pl.ds(offset, half)],
+                        send_sem=send_sem.at[phase, lane, k],
+                        recv_sem=recv_sem.at[phase, lane, k],
+                        device_id=partner(stage),
+                        device_id_type=MESH,
+                    )
+                    flying[lane].start()
+                    sent.append(flying[lane])
+            offset += half
+        return sent
+
+    def fold(x):
+        total = x[:, :128]
+        for i in range(1, x.shape[1] // 128):
+            total = total + x[:, i * 128 : (i + 1) * 128]
+        return total
+
+    def across(x):
+        return jnp.sum(x, axis=1, keepdims=True)
+
+    def times(a, block):
+        return lax.dot_general(
+            a.astype(jnp.bfloat16), block, (((1,), (1,)), ((), ())), preferred_element_type=jnp.float32
+        )
+
+    def blocks(body, init):
+        def step(i, carry):
+            return body(pl.ds(pl.multiple_of(i * BLOCK, BLOCK), BLOCK), carry)
+
+        return lax.fori_loop(0, width // BLOCK, step, init)
+
+    zero = jnp.zeros((count, 128), jnp.float32)
+    none = jnp.zeros((count, grads.shape[0]), jnp.float32)
+
+    sent = gather(t, 0, lambda lane: firsts[lane].wait())
+    for copy in loads:
+        copy.wait()
+
+    def first(at, carry):
+        proj, square = carry
+        d = t[:, at]
+        return proj + times(d, g[:, at]), square + fold(d * d)
+
+    proj, square = blocks(first, (none, zero))
+    norm = across(square)
+    back = proj.astype(jnp.bfloat16)
+
+    def spread(at, carry):
+        acc[:, at] = jnp.dot(back, g[:, at], preferred_element_type=jnp.float32)
+        return carry
+
+    blocks(spread, 0)
+    sent += scatter(1)
+
+    def ready(lane):
+        at = pl.ds(pl.multiple_of(place[lane] * chunk, chunk), chunk)
+        img[rows[lane], at] = acc[rows[lane], at]
+
+    sent += gather(img, 2, ready)
+    for copy in sent:
+        copy.wait_send()
+
+    def image(at):
+        return img[:, at] * (1.0 / n_total) + damping * t[:, at]
+
+    alpha = norm / across(blocks(lambda at, c: c + fold(t[:, at] * image(at)), zero))
+
+    def shrink(at, carry):
+        r = t[:, at] - alpha * image(at)
+        img[:, at] = r
+        return carry + fold(r * r)
+
+    after = across(blocks(shrink, zero))
+    beta = after / norm
+
+    def second(at, carry):
+        proj, square = carry
+        d = img[:, at] + beta * t[:, at]
+        img[:, at] = d
+        return proj + times(d, g[:, at]), square + fold(d * d)
+
+    proj, square = blocks(second, (none, zero))
+    curv = jnp.broadcast_to(across(proj * proj.astype(jnp.bfloat16).astype(jnp.float32)), (count, 128))
+    sent = []
+    for k, stage in enumerate(orders[0]):
+        mail[0, k] = curv
+        copy = pltpu.make_async_remote_copy(
+            src_ref=mail.at[0, k],
+            dst_ref=mail.at[1, k],
+            send_sem=csend.at[k],
+            recv_sem=crecv.at[k],
+            device_id=partner(stage),
+            device_id_type=MESH,
+        )
+        copy.start()
+        copy.wait()
+        curv = curv + mail[1, k]
+    step = after / (curv[:, :1] * (1.0 / n_total) + damping * across(square))
+
+    def last(at, total):
+        x = alpha * t[:, at] + step * img[:, at]
+        acc[:, at] = x
+        return total + times(x, g[:, at])
+
+    scores[...] = blocks(last, none) * width ** (-0.5)
+    z = 0
+    for stage in low:
+        z = z * 2 + bit(stage)
+    for s in range(nr):
+        out[:, pl.ds(s * chunk, chunk)] = acc[:, pl.ds(pl.multiple_of((s * nc + z) * chunk, chunk), chunk)]
+
+
+def per_device(nr, nc, grads, tests):
+    n = nr * nc
+    count, own = tests.shape
+    held, width = grads.shape
+    stages = bits_of(n)
+    if n != 2**stages or nr < 2 or width % (128 * n) or width % BLOCK or count % (8 * LANES):
+        return plain(grads, tests)
+    whole = pltpu.VMEM((count, width), jnp.float32)
+    return pl.pallas_call(
+        functools.partial(kernel, nr, nc),
+        out_shape=(
+            jax.ShapeDtypeStruct((count, own), jnp.float32),
+            jax.ShapeDtypeStruct((count, held), jnp.float32),
+        ),
+        in_specs=[pl.BlockSpec(memory_space=pl.ANY)] * 2,
+        out_specs=[pl.BlockSpec(memory_space=pltpu.VMEM)] * 2,
+        scratch_shapes=[
+            pltpu.VMEM((held, width), jnp.bfloat16),
+            whole,
+            whole,
+            whole,
+            whole,
+            pltpu.VMEM((2, stages, count, 128), jnp.float32),
+            pltpu.SemaphoreType.DMA((n,)),
+            pltpu.SemaphoreType.DMA((LANES,)),
+            pltpu.SemaphoreType.DMA((3, LANES, stages)),
+            pltpu.SemaphoreType.DMA((3, LANES, stages)),
+            pltpu.SemaphoreType.DMA((stages,)),
+            pltpu.SemaphoreType.DMA((stages,)),
+        ],
+        compiler_params=pltpu.CompilerParams(
+            collective_id=0, has_side_effects=True, vmem_limit_bytes=48 * 2**20
+        ),
+    )(grads, tests)
+
+
 def solution(mesh):
     placed = (P(("rows", "cols"), None), P(None, "cols"))
     return jax.shard_map(
-        per_device,
+        functools.partial(per_device, mesh.shape["rows"], mesh.shape["cols"]),
         mesh=mesh,
         in_specs=placed,
         out_specs=(P(None, "cols"), P(None, ("rows", "cols"))),

time: 262 us -> 97 us (0.37)
  waiting for transfers between devices: 184 us -> 0 us
  Pallas kernels: 0 us -> 91.3 us
  blocking collectives: 38.9 us -> 0 us
  matrix products: 13.8 us -> 0 us
  between operations: 14.1 us -> 0.65 us
  other arithmetic: 9.47 us -> 0 us
  local copies, waits for them, and re-layouts: 0.86 us -> 4.81 us
    psum x1 -> x0, waiting for transfers between devices: 134 us -> none  [per_device(): lax.psum(partial_value, ('rows', 'cols')) / n_total + damping * direction]
    pallas_call x0 -> x1, Pallas kernels: none -> 91.3 us  [per_device(): pl.pallas_call(functools.partial(kernel, nr, nc), out_shape=(jax.ShapeDty...]
    all_gather x1 -> x0, waiting for transfers between devices: 50 us -> none  [per_device(): direction = lax.all_gather(tests, 'cols', axis=1, tiled=True)]
    psum x1 -> x0, blocking collectives: 38.9 us -> none  [per_device(): lax.psum(jnp.sum(proj * proj.astype(jnp.bfloat16).astype(jnp.float32), ax...]
    dot_general x3 -> x0, matrix products: 13.8 us -> none  [the longest x1 9.67 us: per_device(): lax.dot_general(project(direction).astype(jnp.bfloat16), grads, (((0,), (...]
    reduce_sum x3 -> x0, other arithmetic: 7.13 us -> none  [the longest x1 2.49 us: per_device(): curv = curv / n_total + damping * jnp.sum(direction * direction, axis=1)]
    unnamed x10 -> x6, local copies, waits for them, and re-layouts: 0.03 us -> 4.81 us
  transfers between devices with their start and end apart: 2 -> 0, of which waited for: 2 -> 0; matrix products, arithmetic and copies ran while one was open for 0% -> 0% of each run, Pallas kernels for 0% -> 0%
where the time goes in v2:
time: 97 us; the launch traced here: 96.8 us
  Pallas kernels  91.3 us (94%)
  local copies, waits for them, and re-layouts  4.81 us (5%)
    pallas_call x1, Pallas kernels, per_device(): pl.pallas_call(functools.partial(kernel, nr, nc), out_shape=(jax.ShapeDty...  91.3 us
    unnamed x6, local copies, waits for them, and re-layouts  4.81 us

profile of v2, /device:TPU:0, one launch (start us, length us, event | category | flops | bytes accessed | tf_op | source)
XLA Modules:
  0.0 96.8 jit_solution(1594168996526466020)
XLA Ops:
  0.6 0.0 copy-start
  0.6 2.3 %copy-done = bf16[288,8192]{1,0:T(8,128)(2,1)S(1)} copy-done((bf16[288,8192]{1,0:T(8,128)(2,1)S(1)}, bf16[288,8192]{1,0:T(8,128)(2,1)}, u32[]{:S(2)}) %copy-start) | copy-done | bytes 4718616
  3.0 0.0 copy-start.1
  3.0 1.0 %copy-done.1 = f32[64,2048]{1,0:T(8,128)S(1)} copy-done((f32[64,2048]{1,0:T(8,128)S(1)}, f32[64,2048]{1,0:T(8,128)}, u32[]{:S(2)}) %copy-start.1) | copy-done | bytes 524312
  4.0 91.3 %shard_map.41 = (f32[64,2048]{1,0:T(8,128)S(1)}, f32[64,288]{1,0:T(8,128)S(1)}) custom-call(bf16[288,8192]{1,0:T(8,128)(2,1)S(1)} %copy-done, f32[64,2048]{1,0:T(8,128)S(1)} %copy-done.1), custom_call_target="tpu_custom_call" | custom-call | tf_op jit(solution)/shard_map/pallas_call | solution.py:278
  95.3 0.8 copy.6
  96.1 0.6 copy.7
Async XLA Ops:
  0.6 2.3 %copy-start = (bf16[288,8192]{1,0:T(8,128)(2,1)S(1)}, bf16[288,8192]{1,0:T(8,128)(2,1)}, u32[]{:S(2)}) copy-start(bf16[288,8192]{1,0:T(8,128)(2,1)} %grads.1) | copy-start | bytes 14155780
  3.0 1.0 %copy-start.1 = (f32[64,2048]{1,0:T(8,128)S(1)}, f32[64,2048]{1,0:T(8,128)}, u32[]{:S(2)}) copy-start(f32[64,2048]{1,0:T(8,128)} %tests.1) | copy-start | bytes 1572868

commit v3 on v2

--- a/solution.py
+++ b/solution.py
@@ -67,8 +67,12 @@
     span = count // LANES
     rest = list(range(1, bits_of(nr)))
     low = [("cols", b) for b in range(bits_of(nc))]
-    orders = [[("rows", b) for b in [0] + r] + low for r in (rest, rest[::-1])]
+    core = [("rows", 0)]
+    far = [("rows", b) for b in rest]
+    orders = [core + far + low, core + far[::-1] + low]
     stages = len(orders[0])
+    far = far + low
+    turns = [core + far[k:3] + far[:k] + far[3:] for k in range(3)]
 
     def bit(stage):
         axis, b = stage
@@ -88,17 +92,24 @@
         )
         loads[-1].start()
 
-    rows = [pl.ds(lane * span, span) for lane in range(LANES)]
-    place = []
-    firsts = []
-    for lane, order in enumerate(orders):
+    def placed(order):
         v = 0
         for stage in order:
             v = v * 2 + bit(stage)
-        place.append(v)
+        return v
+
+    lanes = [(pl.ds(lane * span, span), order, placed(order)) for lane, order in enumerate(orders)]
+    turned = []
+    at = 0
+    for k, order in enumerate(turns):
+        size = 8 * ((count // 8 + 2 - k) // 3)
+        turned.append((pl.ds(at, size), order, placed(order)))
+        at += size
+    firsts = []
+    for lane, (rows, order, v) in enumerate(lanes):
         copy = pltpu.make_async_copy(
-            tests.at[rows[lane], pl.ds(pl.multiple_of(lax.div(v, nc) * chunk, chunk), chunk)],
-            t.at[rows[lane], pl.ds(pl.multiple_of(v * chunk, chunk), chunk)],
+            tests.at[rows, pl.ds(pl.multiple_of(lax.div(v, nc) * chunk, chunk), chunk)],
+            t.at[rows, pl.ds(pl.multiple_of(v * chunk, chunk), chunk)],
             own_sem.at[lane],
         )
         copy.start()
@@ -109,19 +120,19 @@
         pl.semaphore_signal(barrier, inc=1, device_id=partner(stage), device_id_type=MESH)
     pl.semaphore_wait(barrier, stages)
 
-    def gather(buf, phase, ready):
+    def gather(buf, phase, lanes, ready):
         sent = []
-        start = list(place)
-        flying = [None] * LANES
+        start = [v for _, _, v in lanes]
+        flying = [None] * len(lanes)
         for k in range(stages):
             size = chunk * 2**k
-            for lane in range(LANES):
-                stage = orders[lane][stages - 1 - k]
+            for lane, (rows, order, _) in enumerate(lanes):
+                stage = order[stages - 1 - k]
                 if k == 0:
                     ready(lane)
                 else:
                     flying[lane].wait_recv()
-                part = buf.at[rows[lane], pl.ds(pl.multiple_of(start[lane] * chunk, size), size)]
+                part = buf.at[rows, pl.ds(pl.multiple_of(start[lane] * chunk, size), size)]
                 flying[lane] = pltpu.make_async_remote_copy(
                     src_ref=part,
                     dst_ref=part,
@@ -133,29 +144,27 @@
                 flying[lane].start()
                 sent.append(flying[lane])
                 start[lane] = start[lane] - bit(stage) * 2**k
-        for copy in flying:
-            copy.wait_recv()
-        return sent
-
-    def scatter(phase):
+        return sent, flying
+
+    def scatter(phase, lanes, between):
         sent = []
-        start = [0] * LANES
-        flying = [None] * LANES
+        start = [0] * len(lanes)
+        flying = [None] * len(lanes)
         offset = 0
         for k in range(stages + 1):
             half = width // 2 ** (k + 1)
-            for lane in range(LANES):
+            for lane, (rows, order, _) in enumerate(lanes):
                 if k:
                     flying[lane].wait_recv()
                     at = pl.ds(pl.multiple_of(start[lane], 2 * half), 2 * half)
-                    acc[rows[lane], at] = acc[rows[lane], at] + box[rows[lane], pl.ds(offset - 2 * half, 2 * half)]
+                    acc[rows, at] = acc[rows, at] + box[rows, pl.ds(offset - 2 * half, 2 * half)]
                 if k < stages:
-                    stage = orders[lane][k]
+                    stage = order[k]
                     give = start[lane] + (1 - bit(stage)) * half
                     start[lane] = start[lane] + bit(stage) * half
                     flying[lane] = pltpu.make_async_remote_copy(
-                        src_ref=acc.at[rows[lane], pl.ds(pl.multiple_of(give, half), half)],
-                        dst_ref=box.at[rows[lane], pl.ds(offset, half)],
+                        src_ref=acc.at[rows, pl.ds(pl.multiple_of(give, half), half)],
+                        dst_ref=box.at[rows, pl.ds(offset, half)],
                         send_sem=send_sem.at[phase, lane, k],
                         recv_sem=recv_sem.at[phase, lane, k],
                         device_id=partner(stage),
@@ -163,6 +172,8 @@
                     )
                     flying[lane].start()
                     sent.append(flying[lane])
+            if k == 0:
+                between()
             offset += half
         return sent
 
@@ -180,16 +191,20 @@
             a.astype(jnp.bfloat16), block, (((1,), (1,)), ((), ())), preferred_element_type=jnp.float32
         )
 
-    def blocks(body, init):
+    def blocks(body, init, begin=0, size=width):
         def step(i, carry):
-            return body(pl.ds(pl.multiple_of(i * BLOCK, BLOCK), BLOCK), carry)
-
-        return lax.fori_loop(0, width // BLOCK, step, init)
+            return body(pl.ds(pl.multiple_of(begin + i * BLOCK, BLOCK), BLOCK), carry)
+
+        return lax.fori_loop(0, size // BLOCK, step, init)
+
+    half = width // 2
+    mine = bit(core[0]) * half
+    other = half - mine
 
     zero = jnp.zeros((count, 128), jnp.float32)
     none = jnp.zeros((count, grads.shape[0]), jnp.float32)
 
-    sent = gather(t, 0, lambda lane: firsts[lane].wait())
+    sent, flying = gather(t, 0, lanes, lambda lane: firsts[lane].wait())
     for copy in loads:
         copy.wait()
 
@@ -198,7 +213,10 @@
         d = t[:, at]
         return proj + times(d, g[:, at]), square + fold(d * d)
 
-    proj, square = blocks(first, (none, zero))
+    carry = blocks(first, (none, zero), mine, half)
+    for copy in flying:
+        copy.wait_recv()
+    proj, square = blocks(first, carry, other, half)
     norm = across(square)
     back = proj.astype(jnp.bfloat16)
 
@@ -206,21 +224,28 @@
         acc[:, at] = jnp.dot(back, g[:, at], preferred_element_type=jnp.float32)
         return carry
 
-    blocks(spread, 0)
-    sent += scatter(1)
+    blocks(spread, 0, other, half)
+    sent += scatter(1, turned, lambda: blocks(spread, 0, mine, half))
 
     def ready(lane):
-        at = pl.ds(pl.multiple_of(place[lane] * chunk, chunk), chunk)
-        img[rows[lane], at] = acc[rows[lane], at]
-
-    sent += gather(img, 2, ready)
-    for copy in sent:
-        copy.wait_send()
+        rows, _, v = turned[lane]
+        at = pl.ds(pl.multiple_of(v * chunk, chunk), chunk)
+        img[rows, at] = acc[rows, at]
+
+    more, flying = gather(img, 2, turned, ready)
 
     def image(at):
         return img[:, at] * (1.0 / n_total) + damping * t[:, at]
 
-    alpha = norm / across(blocks(lambda at, c: c + fold(t[:, at] * image(at)), zero))
+    def inner(at, carry):
+        return carry + fold(t[:, at] * image(at))
+
+    carry = blocks(inner, zero, mine, half)
+    for copy in flying:
+        copy.wait_recv()
+    alpha = norm / across(blocks(inner, carry, other, half))
+    for copy in sent + more:
+        copy.wait_send()
 
     def shrink(at, carry):
         r = t[:, at] - alpha * image(at)
@@ -272,7 +297,7 @@
     count, own = tests.shape
     held, width = grads.shape
     stages = bits_of(n)
-    if n != 2**stages or nr < 2 or width % (128 * n) or width % BLOCK or count % (8 * LANES):
+    if n != 2**stages or width % (128 * n) or width % (2 * BLOCK) or count % (8 * LANES) or count < 24 or nr < 4 or nc < 2:
         return plain(grads, tests)
     whole = pltpu.VMEM((count, width), jnp.float32)
     return pl.pallas_call(
@@ -292,8 +317,8 @@
             pltpu.VMEM((2, stages, count, 128), jnp.float32),
             pltpu.SemaphoreType.DMA((n,)),
             pltpu.SemaphoreType.DMA((LANES,)),
-            pltpu.SemaphoreType.DMA((3, LANES, stages)),
-            pltpu.SemaphoreType.DMA((3, LANES, stages)),
+            pltpu.SemaphoreType.DMA((3, 3, stages)),
+            pltpu.SemaphoreType.DMA((3, 3, stages)),
             pltpu.SemaphoreType.DMA((stages,)),
             pltpu.SemaphoreType.DMA((stages,)),
         ],

time: 97 us -> 93.6 us (0.965)
  Pallas kernels: 91.3 us -> 87.9 us
    pallas_call x1, Pallas kernels: 91.3 us -> 87.9 us  [per_device(): pl.pallas_call(functools.partial(kernel, nr, nc), out_shape=(jax.ShapeDty...]
where the time goes in v3:
time: 93.6 us; the launch traced here: 93.4 us
  Pallas kernels  87.9 us (94%)
  local copies, waits for them, and re-layouts  4.81 us (5%)
    pallas_call x1, Pallas kernels, per_device(): pl.pallas_call(functools.partial(kernel, nr, nc), out_shape=(jax.ShapeDty...  87.9 us
    unnamed x6, local copies, waits for them, and re-layouts  4.81 us

profile of v3, /device:TPU:0, one launch (start us, length us, event | category | flops | bytes accessed | tf_op | source)
XLA Modules:
  0.0 93.4 jit_solution(13261935751407139866)
XLA Ops:
  0.6 0.0 copy-start
  0.6 2.3 %copy-done = bf16[288,8192]{1,0:T(8,128)(2,1)S(1)} copy-done((bf16[288,8192]{1,0:T(8,128)(2,1)S(1)}, bf16[288,8192]{1,0:T(8,128)(2,1)}, u32[]{:S(2)}) %copy-start) | copy-done | bytes 4718616
  3.0 0.0 copy-start.1
  3.0 1.0 %copy-done.1 = f32[64,2048]{1,0:T(8,128)S(1)} copy-done((f32[64,2048]{1,0:T(8,128)S(1)}, f32[64,2048]{1,0:T(8,128)}, u32[]{:S(2)}) %copy-start.1) | copy-done | bytes 524312
  4.0 87.9 %shard_map.41 = (f32[64,2048]{1,0:T(8,128)S(1)}, f32[64,288]{1,0:T(8,128)S(1)}) custom-call(bf16[288,8192]{1,0:T(8,128)(2,1)S(1)} %copy-done, f32[64,2048]{1,0:T(8,128)S(1)} %copy-done.1), custom_call_target="tpu_custom_call" | custom-call | tf_op jit(solution)/shard_map/pallas_call | solution.py:303
  91.9 0.8 copy.6
  92.7 0.6 copy.7
Async XLA Ops:
  0.6 2.3 %copy-start = (bf16[288,8192]{1,0:T(8,128)(2,1)S(1)}, bf16[288,8192]{1,0:T(8,128)(2,1)}, u32[]{:S(2)}) copy-start(bf16[288,8192]{1,0:T(8,128)(2,1)} %grads.1) | copy-start | bytes 14155780
  3.0 1.0 %copy-start.1 = (f32[64,2048]{1,0:T(8,128)S(1)}, f32[64,2048]{1,0:T(8,128)}, u32[]{:S(2)}) copy-start(f32[64,2048]{1,0:T(8,128)} %tests.1) | copy-start | bytes 1572868

commit v4 on v3

--- a/solution.py
+++ b/solution.py
@@ -116,9 +116,18 @@
         firsts.append(copy)
 
     barrier = pltpu.get_barrier_semaphore()
-    for stage in orders[0]:
-        pl.semaphore_signal(barrier, inc=1, device_id=partner(stage), device_id_type=MESH)
-    pl.semaphore_wait(barrier, stages)
+    row, col = me["rows"], me["cols"]
+    groups = [
+        (2, lax.rem(row, 2), lambda p: {"rows": row - lax.rem(row, 2) + p}),
+        (nr // 2, lax.div(row, 2), lambda p: {"rows": p * 2 + lax.rem(row, 2)}),
+        (nc, col, lambda p: {"cols": p}),
+    ]
+    greeted = 0
+    for m, digit, device in groups:
+        for d in range(1, m):
+            pl.semaphore_signal(barrier, inc=1, device_id=device(lax.rem(digit + d, m)), device_id_type=MESH)
+            greeted += 1
+    pl.semaphore_wait(barrier, greeted)
 
     def gather(buf, phase, lanes, ready):
         sent = []
@@ -264,19 +273,28 @@
     proj, square = blocks(second, (none, zero))
     curv = jnp.broadcast_to(across(proj * proj.astype(jnp.bfloat16).astype(jnp.float32)), (count, 128))
     sent = []
-    for k, stage in enumerate(orders[0]):
-        mail[0, k] = curv
-        copy = pltpu.make_async_remote_copy(
-            src_ref=mail.at[0, k],
-            dst_ref=mail.at[1, k],
-            send_sem=csend.at[k],
-            recv_sem=crecv.at[k],
-            device_id=partner(stage),
-            device_id_type=MESH,
-        )
-        copy.start()
-        copy.wait()
-        curv = curv + mail[1, k]
+    for k, (m, digit, device) in enumerate(groups):
+        mail[k, digit] = curv
+        flying = []
+        for d in range(1, m):
+            copy = pltpu.make_async_remote_copy(
+                src_ref=mail.at[k, digit],
+                dst_ref=mail.at[k, digit],
+                send_sem=csend.at[k, d],
+                recv_sem=crecv.at[k, d],
+                device_id=device(lax.rem(digit + d, m)),
+                device_id_type=MESH,
+            )
+            copy.start()
+            flying.append(copy)
+        for copy in flying:
+            copy.wait_recv()
+        sent += flying
+        curv = mail[k, 0]
+        for p in range(1, m):
+            curv = curv + mail[k, p]
+    for copy in sent:
+        copy.wait_send()
     step = after / (curv[:, :1] * (1.0 / n_total) + damping * across(square))
 
     def last(at, total):
@@ -297,6 +315,7 @@
     count, own = tests.shape
     held, width = grads.shape
     stages = bits_of(n)
+    widest = max(nr // 2, nc)
     if n != 2**stages or width % (128 * n) or width % (2 * BLOCK) or count % (8 * LANES) or count < 24 or nr < 4 or nc < 2:
         return plain(grads, tests)
     whole = pltpu.VMEM((count, width), jnp.float32)
@@ -314,13 +333,13 @@
             whole,
             whole,
             whole,
-            pltpu.VMEM((2, stages, count, 128), jnp.float32),
+            pltpu.VMEM((3, widest, count, 128), jnp.float32),
             pltpu.SemaphoreType.DMA((n,)),
             pltpu.SemaphoreType.DMA((LANES,)),
             pltpu.SemaphoreType.DMA((3, 3, stages)),
             pltpu.SemaphoreType.DMA((3, 3, stages)),
-            pltpu.SemaphoreType.DMA((stages,)),
-            pltpu.SemaphoreType.DMA((stages,)),
+            pltpu.SemaphoreType.DMA((3, widest)),
+            pltpu.SemaphoreType.DMA((3, widest)),
         ],
         compiler_params=pltpu.CompilerParams(
             collective_id=0, has_side_effects=True, vmem_limit_bytes=48 * 2**20

time: 93.6 us -> 88.7 us (0.948)
  Pallas kernels: 87.9 us -> 83.1 us
    pallas_call x1, Pallas kernels: 87.9 us -> 83.1 us  [per_device(): pl.pallas_call(functools.partial(kernel, nr, nc), out_shape=(jax.ShapeDty...]
where the time goes in v4:
time: 88.7 us; the launch traced here: 88.5 us
  Pallas kernels  83.1 us (94%)
  local copies, waits for them, and re-layouts  4.81 us (5%)
    pallas_call x1, Pallas kernels, per_device(): pl.pallas_call(functools.partial(kernel, nr, nc), out_shape=(jax.ShapeDty...  83.1 us
    unnamed x6, local copies, waits for them, and re-layouts  4.81 us

profile of v4, /device:TPU:0, one launch (start us, length us, event | category | flops | bytes accessed | tf_op | source)
XLA Modules:
  0.0 88.5 jit_solution(6423587383432304273)
XLA Ops:
  0.6 0.0 copy-start
  0.6 2.3 %copy-done = bf16[288,8192]{1,0:T(8,128)(2,1)S(1)} copy-done((bf16[288,8192]{1,0:T(8,128)(2,1)S(1)}, bf16[288,8192]{1,0:T(8,128)(2,1)}, u32[]{:S(2)}) %copy-start) | copy-done | bytes 4718616
  3.0 0.0 copy-start.1
  3.0 1.0 %copy-done.1 = f32[64,2048]{1,0:T(8,128)S(1)} copy-done((f32[64,2048]{1,0:T(8,128)S(1)}, f32[64,2048]{1,0:T(8,128)}, u32[]{:S(2)}) %copy-start.1) | copy-done | bytes 524312
  4.0 83.1 %shard_map.41 = (f32[64,2048]{1,0:T(8,128)S(1)}, f32[64,288]{1,0:T(8,128)S(1)}) custom-call(bf16[288,8192]{1,0:T(8,128)(2,1)S(1)} %copy-done, f32[64,2048]{1,0:T(8,128)S(1)} %copy-done.1), custom_call_target="tpu_custom_call" | custom-call | tf_op jit(solution)/shard_map/pallas_call | solution.py:322
  87.1 0.8 copy.6
  87.9 0.6 copy.7
Async XLA Ops:
  0.6 2.3 %copy-start = (bf16[288,8192]{1,0:T(8,128)(2,1)S(1)}, bf16[288,8192]{1,0:T(8,128)(2,1)}, u32[]{:S(2)}) copy-start(bf16[288,8192]{1,0:T(8,128)(2,1)} %grads.1) | copy-start | bytes 14155780
  3.0 1.0 %copy-start.1 = (f32[64,2048]{1,0:T(8,128)S(1)}, f32[64,2048]{1,0:T(8,128)}, u32[]{:S(2)}) copy-start(f32[64,2048]{1,0:T(8,128)} %tests.1) | copy-start | bytes 1572868

commit v5 on v4

--- a/solution.py
+++ b/solution.py
@@ -132,17 +132,37 @@
     def gather(buf, phase, lanes, ready):
         sent = []
         start = [v for _, _, v in lanes]
-        flying = [None] * len(lanes)
-        for k in range(stages):
+        flying = [[] for _ in lanes]
+        done = 0
+        if phase == 0:
+            done = bits_of(nc)
+            for lane, (rows, _, v) in enumerate(lanes):
+                ready(lane)
+                part = buf.at[rows, pl.ds(pl.multiple_of(v * chunk, chunk), chunk)]
+                for d in range(1, nc):
+                    copy = pltpu.make_async_remote_copy(
+                        src_ref=part,
+                        dst_ref=part,
+                        send_sem=send_sem.at[3, lane, d],
+                        recv_sem=recv_sem.at[3, lane, d],
+                        device_id={"cols": lax.rem(col + d, nc)},
+                        device_id_type=MESH,
+                    )
+                    copy.start()
+                    flying[lane].append(copy)
+                    sent.append(copy)
+                start[lane] = v - lax.rem(v, nc)
+        for k in range(done, stages):
             size = chunk * 2**k
             for lane, (rows, order, _) in enumerate(lanes):
                 stage = order[stages - 1 - k]
                 if k == 0:
                     ready(lane)
                 else:
-                    flying[lane].wait_recv()
+                    for copy in flying[lane]:
+                        copy.wait_recv()
                 part = buf.at[rows, pl.ds(pl.multiple_of(start[lane] * chunk, size), size)]
-                flying[lane] = pltpu.make_async_remote_copy(
+                copy = pltpu.make_async_remote_copy(
                     src_ref=part,
                     dst_ref=part,
                     send_sem=send_sem.at[phase, lane, k],
@@ -150,10 +170,11 @@
                     device_id=partner(stage),
                     device_id_type=MESH,
                 )
-                flying[lane].start()
-                sent.append(flying[lane])
+                copy.start()
+                flying[lane] = [copy]
+                sent.append(copy)
                 start[lane] = start[lane] - bit(stage) * 2**k
-        return sent, flying
+        return sent, [copy for copies in flying for copy in copies]
 
     def scatter(phase, lanes, between):
         sent = []
@@ -336,8 +357,8 @@
             pltpu.VMEM((3, widest, count, 128), jnp.float32),
             pltpu.SemaphoreType.DMA((n,)),
             pltpu.SemaphoreType.DMA((LANES,)),
-            pltpu.SemaphoreType.DMA((3, 3, stages)),
-            pltpu.SemaphoreType.DMA((3, 3, stages)),
+            pltpu.SemaphoreType.DMA((4, 3, max(stages, nc))),
+            pltpu.SemaphoreType.DMA((4, 3, max(stages, nc))),
             pltpu.SemaphoreType.DMA((3, widest)),
             pltpu.SemaphoreType.DMA((3, widest)),
         ],

time: 88.7 us -> 88.3 us (level)
  no operation moved by 1% of the time
where the time goes in v5:
time: 88.3 us; the launch traced here: 88.1 us
  Pallas kernels  82.7 us (94%)
  local copies, waits for them, and re-layouts  4.81 us (5%)
    pallas_call x1, Pallas kernels, per_device(): pl.pallas_call(functools.partial(kernel, nr, nc), out_shape=(jax.ShapeDty...  82.7 us
    unnamed x6, local copies, waits for them, and re-layouts  4.81 us

profile of v5, /device:TPU:0, one launch (start us, length us, event | category | flops | bytes accessed | tf_op | source)
XLA Modules:
  0.0 88.1 jit_solution(910642705950092010)
XLA Ops:
  0.6 0.0 copy-start
  0.6 2.3 %copy-done = bf16[288,8192]{1,0:T(8,128)(2,1)S(1)} copy-done((bf16[288,8192]{1,0:T(8,128)(2,1)S(1)}, bf16[288,8192]{1,0:T(8,128)(2,1)}, u32[]{:S(2)}) %copy-start) | copy-done | bytes 4718616
  3.0 0.0 copy-start.1
  3.0 1.0 %copy-done.1 = f32[64,2048]{1,0:T(8,128)S(1)} copy-done((f32[64,2048]{1,0:T(8,128)S(1)}, f32[64,2048]{1,0:T(8,128)}, u32[]{:S(2)}) %copy-start.1) | copy-done | bytes 524312
  4.0 82.7 %shard_map.41 = (f32[64,2048]{1,0:T(8,128)S(1)}, f32[64,288]{1,0:T(8,128)S(1)}) custom-call(bf16[288,8192]{1,0:T(8,128)(2,1)S(1)} %copy-done, f32[64,2048]{1,0:T(8,128)S(1)} %copy-done.1), custom_call_target="tpu_custom_call" | custom-call | tf_op jit(solution)/shard_map/pallas_call | solution.py:343
  86.7 0.8 copy.6
  87.5 0.6 copy.7
Async XLA Ops:
  0.6 2.3 %copy-start = (bf16[288,8192]{1,0:T(8,128)(2,1)S(1)}, bf16[288,8192]{1,0:T(8,128)(2,1)}, u32[]{:S(2)}) copy-start(bf16[288,8192]{1,0:T(8,128)(2,1)} %grads.1) | copy-start | bytes 14155780
  3.0 1.0 %copy-start.1 = (f32[64,2048]{1,0:T(8,128)S(1)}, f32[64,2048]{1,0:T(8,128)}, u32[]{:S(2)}) copy-start(f32[64,2048]{1,0:T(8,128)} %tests.1) | copy-start | bytes 1572868
